TPU v7x, 32 devices: a whole 2x2x4 slice. The times are simulated.
32 devices in a mesh: row: 8 (over z, y), col: 4 (over x, core).
Axes of the slice: x: 2, y: 2, z: 4, core: 2. Of those that a mesh axis runs over, the one named last changes fastest.
Arguments:
- tokens: bfloat16 [1600, 8192], P('row', 'col')
- ln1_gain: float32 [1600], P('row'), may hold values from 0.25 to 1.75
- ln1_shift: float32 [1600], P('row'), may hold values from -4 to 4
- weight_qkv: bfloat16 [1600, 4800], P('row', 'col'), may hold values from -0.21875 to 0.21875
- bias_qkv: float32 [4800], P('col'), may hold values from -4 to 4
- weight_out: bfloat16 [1600, 1600], P('row', 'col'), may hold values from -0.625 to 0.625
- bias_out: float32 [1600], P('row'), may hold values from -6 to 6
- ln2_gain: float32 [1600], P('row'), may hold values from 0.25 to 1.75
- ln2_shift: float32 [1600], P('row'), may hold values from -4 to 4
- weight_up: bfloat16 [1600, 6400], P('row', 'col'), may hold values from -0.15625 to 0.15625
- bias_up: float32 [6400], P('col'), may hold values from -6 to 6
- weight_down: bfloat16 [1600, 6400], P('row', 'col'), may hold values from -0.109375 to 0.109375
- bias_down: float32 [1600], P('row'), may hold values from -6 to 6
- cotangent: bfloat16 [1600, 8192], P('row', 'col')
Outputs:
- block_output: bfloat16 [1600, 8192], P('row', 'col')
- grad_tokens: float32 [1600, 8192], P('row', 'col')
- grad_ln1_gain: float32 [1600], P('row')
- grad_ln1_shift: float32 [1600], P('row')
- grad_weight_qkv: float32 [1600, 4800], P('row', 'col')
- grad_bias_qkv: float32 [4800], P('col')
- grad_weight_out: float32 [1600, 1600], P('row', 'col')
- grad_bias_out: float32 [1600], P('row')
- grad_ln2_gain: float32 [1600], P('row')
- grad_ln2_shift: float32 [1600], P('row')
- grad_weight_up: float32 [1600, 6400], P('row', 'col')
- grad_bias_up: float32 [6400], P('col')
- grad_weight_down: float32 [1600, 6400], P('row', 'col')
- grad_bias_down: float32 [1600], P('row')
All inputs are finite; a program needn't handle non-finite values.
Results may differ from a plain program's by a relative error of at most 0.012.
The roundings to bfloat16 on the way count: a program that leaves them out, or rounds other values in their place, can miss the bound.
Values may be sent and summed in bfloat16 or wider, within the bound.
A program may use at most 256 MiB of HBM per device.

v0:
```python
import jax
import jax.numpy as jnp
from jax import lax
from jax.sharding import PartitionSpec as P

D = 1600
H = 25
HD = 64
L = 1024
CHANNELS = 3 * HD
epsilon = 1e-05
excluded = -1e30
TN = (((0,), (0,)), ((), ()))
NN = (((1,), (0,)), ((), ()))
NT = (((1,), (1,)), ((), ()))


def product(left, right, dims):
    return lax.dot_general(left, right, dims, preferred_element_type=jnp.float32)


def norm_stats(values):
    mean = jnp.mean(values, axis=0, keepdims=True)
    centred = values - mean
    scale = lax.rsqrt(jnp.mean(centred * centred, axis=0, keepdims=True) + epsilon)
    return (centred * scale, scale)


def norm_backward(gradient, centred, scale, gain):
    scaled = gradient * gain
    adjusted = (
        scaled
        - jnp.mean(scaled, axis=0, keepdims=True)
        - centred * jnp.mean(scaled * centred, axis=0, keepdims=True)
    )
    return (adjusted * scale, jnp.sum(gradient * centred, axis=1), jnp.sum(gradient, axis=1))


def block_order(rows, cols):
    return [(q * cols + c, c * rows + q) for q in range(rows) for c in range(cols)]


def to_blocks(values, rows, cols):
    k, feats, toks = values.shape
    split = values.reshape(k, feats, rows, toks // rows)
    got = lax.all_to_all(split, "row", split_axis=2, concat_axis=1)
    got = got.reshape(k, rows * feats, toks // rows)
    return lax.ppermute(got, ("row", "col"), block_order(rows, cols))


def from_blocks(values, rows, cols):
    back = [(b, a) for a, b in block_order(rows, cols)]
    got = lax.ppermute(values, ("row", "col"), back)
    feats, toks = values.shape
    got = got.reshape(rows, feats // rows, toks)
    got = lax.all_to_all(got, "row", split_axis=0, concat_axis=1)
    return got.reshape(feats // rows, rows * toks)


def regroup_matrix(channels, slots, cols):
    source = jnp.arange(channels * H, dtype=jnp.int32)
    channel, head = (source // H, source % H)
    target = (head % cols * slots + head // cols) * channels + channel
    return (
        target[:, None] == jnp.arange(cols * slots * channels, dtype=jnp.int32)[None, :]
    ).astype(jnp.bfloat16)


def group_heads(weight, matrix, cols):
    moved = product(weight, matrix, NN).astype(jnp.bfloat16)
    moved = moved.reshape(moved.shape[0], cols, -1)
    got = lax.all_to_all(moved, "col", split_axis=1, concat_axis=1, tiled=True)
    return got.reshape(got.shape[0], -1)


def ungroup_heads(gradient, matrix, cols):
    moved = gradient.reshape(gradient.shape[0], cols, -1)
    got = lax.all_to_all(moved, "col", split_axis=1, concat_axis=1, tiled=True)
    return product(got.reshape(got.shape[0], -1), matrix, NT)


def head_rows(values, cols, slots):
    rest = values.shape[1:]
    split = values.reshape(cols, slots, -1, *rest)
    return jnp.moveaxis(split, 0, 1).reshape(slots, -1, *rest)


def flat_rows(values, cols, slots):
    rest = values.shape[2:]
    split = values.reshape(slots, cols, -1, *rest)
    return jnp.moveaxis(split, 0, 1).reshape(-1, *rest)


def attend_forward(heads):
    allowed = jnp.arange(L)[:, None] <= jnp.arange(L)[None, :]
    outs, logs = ([], [])
    for s in range(heads.shape[0]):
        query, key, value = (heads[s, :HD], heads[s, HD : 2 * HD], heads[s, 2 * HD :])
        scores = product(key, query, TN) * HD ** (-0.5)
        scores = jnp.where(allowed, scores, excluded)
        peak = jnp.max(scores, axis=0, keepdims=True)
        weights = jnp.exp(scores - peak)
        total = jnp.sum(weights, axis=0, keepdims=True)
        low = (weights / total).astype(jnp.bfloat16)
        outs.append(product(value, low, NN).astype(jnp.bfloat16))
        logs.append(peak + jnp.log(total))
    return (jnp.stack(outs), jnp.stack(logs))


def attend_backward(heads, grads, logs):
    allowed = jnp.arange(L)[:, None] <= jnp.arange(L)[None, :]
    outs = []
    for s in range(heads.shape[0]):
        query, key, value = (heads[s, :HD], heads[s, HD : 2 * HD], heads[s, 2 * HD :])
        grad = grads[s]
        scores = product(key, query, TN) * HD ** (-0.5)
        scores = jnp.where(allowed, scores, excluded)
        weights = jnp.exp(scores - logs[s])
        grad_value = product(grad, weights.astype(jnp.bfloat16), NT)
        grad_weights = product(value, grad, TN)
        inner = jnp.sum(weights * grad_weights, axis=0, keepdims=True)
        low = (weights * (grad_weights - inner)).astype(jnp.bfloat16)
        grad_query = product(key, low, NN) * HD ** (-0.5)
        grad_key = product(query, low, NT) * HD ** (-0.5)
        outs.append(
            jnp.concatenate([grad_query, grad_key, grad_value], axis=0).astype(jnp.bfloat16)
        )
    return jnp.stack(outs)


def spread(values):
    return lax.all_gather(values, "col", axis=1, tiled=True)


def share(values):
    return lax.psum_scatter(
        values.astype(jnp.bfloat16), "col", scatter_dimension=1, tiled=True
    ).astype(jnp.float32)


def whole_weight(weight):
    return lax.all_gather(weight, "row", axis=0, tiled=True)


def share_weight(gradient):
    return lax.psum_scatter(gradient.astype(jnp.bfloat16), "row", scatter_dimension=0, tiled=True)


def body(
    tokens,
    ln1_gain,
    ln1_shift,
    weight_qkv,
    bias_qkv,
    weight_out,
    bias_out,
    ln2_gain,
    ln2_shift,
    weight_up,
    bias_up,
    weight_down,
    bias_down,
    cotangent,
):
    rows, cols = (lax.axis_size("row"), lax.axis_size("col"))
    row, col = (lax.axis_index("row"), lax.axis_index("col"))
    slots = (H + cols - 1) // cols
    qkv_channels = CHANNELS // cols
    out_channels = HD // cols
    vectors = lax.all_gather(
        jnp.stack([ln1_gain, ln1_shift, bias_out, ln2_gain, ln2_shift, bias_down]),
        "row",
        axis=1,
        tiled=True,
    )[:, :, None]
    gain_one, shift_one, out_bias, gain_two, shift_two, down_bias = vectors
    biases = lax.all_gather(bias_qkv, "col", axis=0, tiled=True).reshape(CHANNELS, H)
    biases = jnp.pad(biases, ((0, 0), (0, slots * cols - H))).reshape(CHANNELS, slots, cols)
    qkv_bias = lax.dynamic_index_in_dim(biases, col, axis=2, keepdims=False).T[:, :, None]
    qkv_matrix = regroup_matrix(qkv_channels, slots, cols)
    out_matrix = regroup_matrix(out_channels, slots, cols)
    qkv_weight = whole_weight(group_heads(weight_qkv, qkv_matrix, cols))
    out_weight = whole_weight(group_heads(weight_out, out_matrix, cols))
    up_weight = whole_weight(weight_up)
    down_weight = whole_weight(weight_down)
    own = to_blocks(jnp.stack([tokens, cotangent]), rows, cols)
    both = lax.all_gather(own, "col", axis=2, tiled=True)
    residual_own = own[0].astype(jnp.float32)
    cot_own = own[1].astype(jnp.float32)
    cot = both[1]
    normed_in = (norm_stats(both[0].astype(jnp.float32))[0] * gain_one + shift_one).astype(
        jnp.bfloat16
    )
    qkv = product(qkv_weight, normed_in, TN)
    heads = (head_rows(qkv, cols, slots) + qkv_bias).astype(jnp.bfloat16)
    attended, logs = attend_forward(heads)
    attended = flat_rows(attended, cols, slots)
    residual_mid = residual_own + share(product(out_weight, attended, NN)) + out_bias
    centred_mid, scale_mid = norm_stats(residual_mid)
    normed_mid = spread((centred_mid * gain_two + shift_two).astype(jnp.bfloat16))
    hidden_pre = product(up_weight, normed_mid, TN) + bias_up[:, None]
    hidden = jax.nn.gelu(hidden_pre, approximate=True).astype(jnp.bfloat16)
    block_output = (residual_mid + share(product(down_weight, hidden, NN)) + down_bias).astype(
        jnp.bfloat16
    )
    block_output = from_blocks(block_output, rows, cols)
    grad_hidden = product(down_weight, cot, TN)
    gelu_back = jax.vjp(lambda inner: jax.nn.gelu(inner, approximate=True), hidden_pre)[1]
    grad_pre = gelu_back(grad_hidden)[0].astype(jnp.bfloat16)
    grad_weight_down = share_weight(product(cot, hidden, NT)).astype(jnp.float32)
    grad_normed_mid = share(product(up_weight, grad_pre, NN))
    grad_weight_up = share_weight(product(normed_mid, grad_pre, NT)).astype(jnp.float32)
    up_part = jnp.sum(grad_pre, axis=1, dtype=jnp.float32)
    grad_norm_mid, gain_two_part, shift_two_part = norm_backward(
        grad_normed_mid, centred_mid, scale_mid, gain_two
    )
    grad_residual_mid = cot_own + grad_norm_mid
    grad_branch_own = grad_residual_mid.astype(jnp.bfloat16)
    grad_branch = spread(grad_branch_own)
    grad_attended = product(out_weight, grad_branch, TN).astype(jnp.bfloat16)
    grad_weight_out = ungroup_heads(
        share_weight(product(grad_branch, attended, NT)), out_matrix, cols
    )
    grad_qkv = attend_backward(heads, head_rows(grad_attended, cols, slots), logs)
    grad_qkv = flat_rows(grad_qkv, cols, slots)
    grad_weight_qkv = ungroup_heads(
        share_weight(product(normed_in, grad_qkv, NT)), qkv_matrix, cols
    )
    qkv_part = jnp.sum(grad_qkv, axis=1, dtype=jnp.float32)
    grad_normed_in = share(product(qkv_weight, grad_qkv, NN))
    centred_in, scale_in = norm_stats(residual_own)
    grad_norm_in, gain_one_part, shift_one_part = norm_backward(
        grad_normed_in, centred_in, scale_in, gain_one
    )
    grad_tokens = from_blocks(grad_residual_mid + grad_norm_in, rows, cols)
    features = jnp.stack(
        [
            gain_one_part,
            shift_one_part,
            jnp.sum(grad_branch_own, axis=1, dtype=jnp.float32),
            gain_two_part,
            shift_two_part,
            jnp.sum(cot_own, axis=1),
        ]
    )
    features = lax.psum(features, ("row", "col"))
    features = lax.dynamic_slice_in_dim(features, row * (D // rows), D // rows, axis=1)
    units = lax.psum(jnp.concatenate([up_part, qkv_part]), "row")
    grad_bias_up = units[: up_part.shape[0]]
    spread_bias = lax.all_gather(
        units[up_part.shape[0] :].reshape(cols, slots, qkv_channels), "col", axis=0
    )
    mine = lax.dynamic_index_in_dim(spread_bias, col, axis=1, keepdims=False)
    grad_bias_qkv = mine.transpose(2, 1, 0).reshape(qkv_channels, slots * cols)[:, :H].reshape(-1)
    return (
        block_output,
        grad_tokens,
        features[0],
        features[1],
        grad_weight_qkv,
        grad_bias_qkv,
        grad_weight_out,
        features[2],
        features[3],
        features[4],
        grad_weight_up,
        grad_bias_up,
        grad_weight_down,
        features[5],
    )


def solution(mesh):
    both, row, col = (P("row", "col"), P("row"), P("col"))
    in_specs = (both, row, row, both, col, both, row, row, row, both, col, both, row, both)
    out_specs = (both, both, row, row, both, col, both, row, row, row, both, col, both, row)
    return jax.shard_map(body, mesh=mesh, in_specs=in_specs, out_specs=out_specs, check_vma=False)
```

profile of v0, /device:TPU:14, one launch (start us, length us, event | category | flops | bytes accessed | tf_op | source)
XLA Modules:
  0.0 1462.5 jit_solution(7190868534278760962)
XLA Ops:
  10.5 11.2 all_to_all.65
  24.3 61.1 %all_to_all.66 = bf16[2,1,200,8,256]{4,2,0,1,3:T(8,128)(2,1)S(1)} all-to-all(bf16[2,1,200,8,256]{4,2,0,1,3:T(8,128)(2,1)S(1)} %copy.106), channel_id=1, replica_groups=mesh['row'=8,'col'=4] {'row'}, dimensions={3} | all-to-all | bytes 3276800 | tf_op jit(solution)/shard_map/all_to_all | solution.py:46
  87.9 102.6 %collective-permute-done = bf16[2,1600,256]{2,1,0:T(8,128)(2,1)S(1)} collective-permute-done((bf16[2,1600,256]{2,1,0:T(8,128)(2,1)S(1)}, bf16[2,1600,256]{2,1,0:T(8,128)(2,1)S(1)}, u32[]{:S(2)}, u32[]{:S(2)}) %collective-permute-start) | collective-permute-done | bytes 1638432 | tf_op jit(solution)/shard_map/ppermute | solution.py:48
  193.0 6.0 all-to-all-start.1
  200.6 11.4 all-reduce.1
  212.4 26.7 %all-gather = f32[8,200,6]{1,2,0:T(8,128)S(1)} all-gather(f32[1,200,6]{1,2,0:T(8,128)S(1)} %bitcast.520), channel_id=1, replica_groups=mesh['row'=8,'col'=4] {'row'}, dimensions={0}, use_global_device_ids=true | all-gather | bytes 43200 | tf_op jit(solution)/shard_map/all_gather | solution.py:170
  240.9 7.5 copy.112
  248.5 2.7 convert_reduce_fusion
  251.2 3.1 fusion.15
  254.4 7.7 fusion.43
  280.9 7.9 all-gather.9.cloned.1.call-done
  288.8 5.1 convolution_convert_fusion.6
  294.5 36.7 %reduce-scatter.15.cloned.1.call-done = bf16[1600,256]{1,0:T(8,128)(2,1)} async-done(((bf16[1600,1024]{1,0:T(8,128)(2,1)}), bf16[1600,256]{1,0:T(8,128)(2,1)}) %reduce-scatter.15.cloned.1.call-update) | async-done | bytes 819216 | tf_op jit(solution)/shard_map/reduce_scatter | solution.py:136
  334.3 3.3 add_convert_fusion.1
  338.4 81.3 %all-gather.17.cloned.1.call-done = bf16[1600,1600]{1,0:T(8,128)(2,1)} async-done(((bf16[200,1600]{1,0:T(8,128)(2,1)}), bf16[1600,1600]{1,0:T(8,128)(2,1)}) %all-gather.17.cloned.1.call-update) | async-done | bytes 5120016 | tf_op jit(solution)/shard_map/all_gather | solution.py:142
  419.7 31.1 %all-gather.15.cloned.1.call-done = bf16[1600,1024]{1,0:T(8,128)(2,1)} async-done(((bf16[1600,256]{1,0:T(8,128)(2,1)}), bf16[1600,1024]{1,0:T(8,128)(2,1)}) %all-gather.15.cloned.1.call-update) | async-done | bytes 3276816 | tf_op jit(solution)/shard_map/all_gather | solution.py:132
  450.8 11.1 fusion.233
  461.9 77.5 %all-gather.19.cloned.1.call-done = bf16[1600,1600]{1,0:T(8,128)(2,1)} async-done(((bf16[200,1600]{1,0:T(8,128)(2,1)}), bf16[1600,1600]{1,0:T(8,128)(2,1)}) %all-gather.19.cloned.1.call-update) | async-done | bytes 5120016 | tf_op jit(solution)/shard_map/all_gather | solution.py:142
  539.4 15.8 %convert_reduce_fusion.1 = (f32[1600]{0:T(1024)}, bf16[1600,1024]{1,0:T(8,128)(2,1)S(1)}) fusion(f32[1024,1600]{0,1:T(8,128)} %fusion.233, f32[1600]{0:T(1024)S(1)} %copy-done.50, bf16[1600,1600]{1,0:T(8,128)(2,1)} %all-gather.19.cloned.1.call-done, bf16[2,1600,1024]{2,1,0:T(8,128)(2,1)} %all-gather.13.cloned.1.call-done), kind=kOutput, calls=%fused_computation.32 | convolution fusion | flops 5280561664 | bytes 18444800 | tf_op jit(solution)/shard_map/dot_general | solution.py:19
  557.0 7.4 fusion.34
  564.9 37.8 %reduce-scatter.19.cloned.1.call-done = bf16[1600,256]{1,0:T(8,128)(2,1)} async-done(((bf16[1600,1024]{1,0:T(8,128)(2,1)}), bf16[1600,256]{1,0:T(8,128)(2,1)}) %reduce-scatter.19.cloned.1.call-update) | async-done | bytes 819216 | tf_op jit(solution)/shard_map/reduce_scatter | solution.py:136
  602.7 2.5 fusion.96
  605.2 3.0 convert_reduce_fusion.7
  608.5 29.5 %all-gather.21.cloned.1.call-done = bf16[1600,1024]{1,0:T(8,128)(2,1)} async-done(((bf16[1600,256]{1,0:T(8,128)(2,1)}), bf16[1600,1024]{1,0:T(8,128)(2,1)}) %all-gather.21.cloned.1.call-update) | async-done | bytes 3276816 | tf_op jit(solution)/shard_map/all_gather | solution.py:132
  638.1 4.4 convolution_convert_fusion.8
  680.2 6.7 convolution_convert_fusion.5
  687.0 11.5 fusion.33
  698.6 5.3 convolution_convert_fusion.7
  704.0 9.7 convolution_convert_fusion.2
  713.9 12.9 convolution_convert_fusion
  726.9 10.3 convolution_convert_fusion.1
  739.6 27.7 %reduce-scatter.17.cloned.1.call-done = bf16[1600,256]{1,0:T(8,128)(2,1)} async-done(((bf16[1600,1024]{1,0:T(8,128)(2,1)}), bf16[1600,256]{1,0:T(8,128)(2,1)}) %reduce-scatter.17.cloned.1.call-update) | async-done | bytes 819216 | tf_op jit(solution)/shard_map/reduce_scatter | solution.py:136
  767.3 4.6 fusion.88
  771.9 4.7 collective-permute-start.1
  776.6 95.2 %reduce-scatter.23.cloned.1.call-done = bf16[200,448]{1,0:T(8,128)(2,1)} async-done(((bf16[1600,448]{1,0:T(8,128)(2,1)}), bf16[200,448]{1,0:T(8,128)(2,1)}) %reduce-scatter.23.cloned.1.call-update) | async-done | bytes 179216 | tf_op jit(solution)/shard_map/reduce_scatter | solution.py:146
  873.0 6.9 all_to_all.67
  879.8 4.6 all-to-all-start.3
  884.4 4.3 collective-permute-start.2
  888.8 192.3 %reduce-scatter.25.cloned.1.call-done = bf16[200,1344]{1,0:T(8,128)(2,1)} async-done(((bf16[1600,1344]{1,0:T(8,128)(2,1)}), bf16[200,1344]{1,0:T(8,128)(2,1)}) %reduce-scatter.25.cloned.1.call-update) | async-done | bytes 537616
  1084.1 4.0 all-to-all-start.5
  1088.1 8.1 all-to-all-done.5
  1097.1 4.5 all-to-all-start.4
  1101.7 132.7 %reduce-scatter.29.cloned.1.call-done = bf16[200,1600]{1,0:T(8,128)(2,1)} async-done(((bf16[1600,1600]{1,0:T(8,128)(2,1)}), bf16[200,1600]{1,0:T(8,128)(2,1)}) %reduce-scatter.29.cloned.1.call-update) | async-done | bytes 640016
  1236.7 123.5 %reduce-scatter.27.cloned.1.call-done = bf16[200,1600]{1,0:T(8,128)(2,1)} async-done(((bf16[1600,1600]{1,0:T(8,128)(2,1)}), bf16[200,1600]{1,0:T(8,128)(2,1)}) %reduce-scatter.27.cloned.1.call-update) | async-done | bytes 640016
  1364.8 29.2 %psum.15 = f32[2944]{0:T(1024)S(1)} all-reduce(f32[2944]{0:T(1024)S(1)} %pad_maximum_fusion.8), channel_id=1, replica_groups=mesh['row'=8,'col'=4] {'row'}, use_global_device_ids=true, to_apply=%region_45.46 | all-reduce | flops 2944 | bytes 23552 | tf_op jit(solution)/shard_map/psum | solution.py:248
  1394.8 5.3 all_gather.39
  1402.4 46.0 %psum.14 = f32[6,1600]{1,0:T(8,128)S(1)} all-reduce(f32[6,1600]{1,0:T(8,128)S(1)} %stack.110), channel_id=1, replica_groups=mesh['row'=8,'col'=4] {'row','col'}, use_global_device_ids=true, to_apply=%region_41.42 | all-reduce | flops 9600 | bytes 76800 | tf_op jit(solution)/shard_map/psum | solution.py:246
  1451.9 2.5 fusion
  (313 shorter events, 99.1 us)
Async XLA Ops:
  7.2 233.7 %all-gather.11.cloned.1.call-start = ((), (), s32[]{:S(2)}) async-start(), calls=%async_computation.16 | async-start | bytes 5068800 | tf_op jit(solution)/shard_map/all_gather | solution.py:142
  9.8 13.5 copy-start.24
  9.8 13.8 copy-start.25
  23.3 225.2 %all-gather.13.cloned.1.call-start = ((), (), s32[]{:S(2)}) async-start(), calls=%async_computation.17 | async-start | bytes 8192000 | tf_op jit(solution)/shard_map/all_gather | solution.py:187
  24.2 167.4 %copy-start.49 = (bf16[200,400]{1,0:T(8,128)(2,1)S(1)}, bf16[200,400]{1,0:T(8,128)(2,1)}, u32[]{:S(2)}) copy-start(bf16[200,400]{1,0:T(8,128)(2,1)} %param.19) | copy-start | bytes 480004
  85.4 113.6 %copy-start.51 = (u32[32]{0:T(128)S(1)}, u32[32]{0:T(128)}, u32[]{:S(2)}) copy-start(u32[32]{0:T(128)} %constant.134) | copy-start | bytes 388
  85.4 114.8 %copy-start.35 = (f32[1200]{0:T(1024)S(1)}, f32[1200]{0:T(1024)}, u32[]{:S(2)}) copy-start(f32[1200]{0:T(1024)} %param.18) | copy-start | bytes 14404
  85.4 126.9 %copy-start.42 = (f32[200]{0:T(256)S(1)}, f32[200]{0:T(256)}, u32[]{:S(2)}) copy-start(f32[200]{0:T(256)} %param.15) | copy-start | bytes 2404
  85.4 126.9 %copy-start.43 = (f32[200]{0:T(256)S(1)}, f32[200]{0:T(256)}, u32[]{:S(2)}) copy-start(f32[200]{0:T(256)} %param.16) | copy-start | bytes 2404
  85.4 126.9 %copy-start.44 = (f32[200]{0:T(256)S(1)}, f32[200]{0:T(256)}, u32[]{:S(2)}) copy-start(f32[200]{0:T(256)} %param.20) | copy-start | bytes 2404
  85.4 126.9 %copy-start.45 = (f32[200]{0:T(256)S(1)}, f32[200]{0:T(256)}, u32[]{:S(2)}) copy-start(f32[200]{0:T(256)} %param.21) | copy-start | bytes 2404
  85.4 126.9 %copy-start.46 = (f32[200]{0:T(256)S(1)}, f32[200]{0:T(256)}, u32[]{:S(2)}) copy-start(f32[200]{0:T(256)} %param.22) | copy-start | bytes 2404
  85.4 126.9 %copy-start.47 = (f32[200]{0:T(256)S(1)}, f32[200]{0:T(256)}, u32[]{:S(2)}) copy-start(f32[200]{0:T(256)} %param.26) | copy-start | bytes 2404
  85.6 104.9 %collective-permute-start = (bf16[2,1600,256]{2,1,0:T(8,128)(2,1)S(1)}, bf16[2,1600,256]{2,1,0:T(8,128)(2,1)S(1)}, u32[]{:S(2)}, u32[]{:S(2)}) collective-permute-start(bf16[2,1600,256]{2,1,0:T(8,128)(2,1)S(1)} %bitcast.483), channel_id=1, source_target_pairs={{0,0},{1,8},{2,16},{3,24},{4,1},{5,9},{6,17},{7,25},{8,2},{9,10},{... | collective-permute-start | bytes 4915208 | tf_op jit(solution)/shard_map/ppermute | solution.py:48
  191.7 47.6 %copy-start.32 = (s32[400]{0:T(512)}, s32[400]{0:T(512)S(1)}, u32[]{:S(2)}) copy-start(s32[400]{0:T(512)S(1)} %fusion.208) | copy-start | bytes 4804
  193.0 46.9 %all-to-all-start.1 = ((bf16[200,4,112]{2,0,1:T(8,128)(2,1)}), bf16[200,4,112]{2,0,1:T(8,128)(2,1)S(1)}, u32[]{:S(2)}, u32[]{:S(2)}) async-start(bf16[200,4,112]{2,0,1:T(8,128)(2,1)} %copy.108), calls=%async_computation.1 | async-start | bytes 409600 | tf_op jit(solution)/shard_map/all_to_all | solution.py:72
  199.0 89.8 %all-gather.9.cloned.1.call-start = ((), (), s32[]{:S(2)}) async-start(), calls=%async_computation.15 | async-start | bytes 1843200 | tf_op jit(solution)/shard_map/all_gather | solution.py:142
  239.9 14.5 copy-start.26
  239.9 14.5 copy-start.38
  240.9 90.4 %reduce-scatter.15.cloned.1.call-start = ((), (), s32[]{:S(2)}) async-start(), calls=%async_computation.18 | async-start | bytes 4096000 | tf_op jit(solution)/shard_map/reduce_scatter | solution.py:136
  251.2 10.9 copy-start.30
  263.4 16.0 %copy-start.19 = (bf16[7,192,1024]{2,1,0:T(8,128)(2,1)}, bf16[7,192,1024]{2,1,0:T(8,128)(2,1)S(1)}, u32[]{:S(2)}) copy-start(bf16[7,192,1024]{2,1,0:T(8,128)(2,1)S(1)} %fusion.20) | copy-start | bytes 8257540
  264.3 12.8 copy-start.4
  280.9 7.9 copy-start.29
  293.9 37.4 %copy-start.3 = (bf16[2,1600,256]{2,1,0:T(8,128)(2,1)S(1)}, bf16[2,1600,256]{2,1,0:T(8,128)(2,1)}, u32[]{:S(2)}) copy-start(bf16[2,1600,256]{2,1,0:T(8,128)(2,1)} %copy-done.2) | copy-start | bytes 4915204
  293.9 125.8 %all-gather.17.cloned.1.call-start = ((), (), s32[]{:S(2)}) async-start(), calls=%async_computation.20 | async-start | bytes 5990400 | tf_op jit(solution)/shard_map/all_gather | solution.py:142
  294.5 156.3 %all-gather.15.cloned.1.call-start = ((), (), s32[]{:S(2)}) async-start(), calls=%async_computation.19 | async-start | bytes 4096000 | tf_op jit(solution)/shard_map/all_gather | solution.py:132
  337.5 201.9 %all-gather.19.cloned.1.call-start = ((), (), s32[]{:S(2)}) async-start(), calls=%async_computation.21 | async-start | bytes 5990400 | tf_op jit(solution)/shard_map/all_gather | solution.py:142
  338.3 201.1 %copy-start.50 = (f32[1600]{0:T(1024)S(1)}, f32[1600]{0:T(1024)}, u32[]{:S(2)}) copy-start(f32[1600]{0:T(1024)} %param.24) | copy-start | bytes 19204
  338.3 264.4 %reduce-scatter.19.cloned.1.call-start = ((), (), s32[]{:S(2)}) async-start(), calls=%async_computation.23 | async-start | bytes 4096000 | tf_op jit(solution)/shard_map/reduce_scatter | solution.py:136
  539.4 17.6 %copy-start.48 = (bf16[1600,1600]{1,0:T(8,128)(2,1)S(1)}, bf16[1600,1600]{1,0:T(8,128)(2,1)}, u32[]{:S(2)}) copy-start(bf16[1600,1600]{1,0:T(8,128)(2,1)} %all-gather.17.cloned.1.call-done) | copy-start | bytes 15360004
  564.5 38.2 %copy-start.18 = (bf16[1600,256]{1,0:T(8,128)(2,1)S(1)}, bf16[1600,256]{1,0:T(8,128)(2,1)}, u32[]{:S(2)}) copy-start(bf16[1600,256]{1,0:T(8,128)(2,1)} %reduce-scatter.15.cloned.1.call-done) | copy-start | bytes 2457604
  564.5 73.6 %all-gather.21.cloned.1.call-start = ((), (), s32[]{:S(2)}) async-start(), calls=%async_computation.24 | async-start | bytes 4096000 | tf_op jit(solution)/shard_map/all_gather | solution.py:132
  608.2 129.1 %reduce-scatter.21.cloned.1.call-start = ((), (), s32[]{:S(2)}) async-start(), calls=%async_computation.25 | async-start | bytes 4096000 | tf_op jit(solution)/shard_map/reduce_scatter | solution.py:136
  686.9 80.4 %reduce-scatter.17.cloned.1.call-start = ((), (), s32[]{:S(2)}) async-start(), calls=%async_computation.22 | async-start | bytes 4096000 | tf_op jit(solution)/shard_map/reduce_scatter | solution.py:136
  698.5 173.3 %reduce-scatter.23.cloned.1.call-start = ((), (), s32[]{:S(2)}) async-start(), calls=%async_computation.26 | async-start | bytes 1843200 | tf_op jit(solution)/shard_map/reduce_scatter | solution.py:146
  703.9 377.2 %reduce-scatter.25.cloned.1.call-start = ((), (), s32[]{:S(2)}) async-start(), calls=%async_computation.27 | async-start | bytes 5068800
  713.7 520.7 %reduce-scatter.29.cloned.1.call-start = ((), (), s32[]{:S(2)}) async-start(), calls=%async_computation.29 | async-start | bytes 5990400
  726.9 633.3 %reduce-scatter.27.cloned.1.call-start = ((), (), s32[]{:S(2)}) async-start(), calls=%async_computation.28 | async-start | bytes 5990400
  737.2 30.1 %copy-start.28 = (f32[1600]{0:T(1024)S(1)}, f32[1600]{0:T(1024)}, u32[]{:S(2)}) copy-start(f32[1600]{0:T(1024)} %get-tuple-element.25) | copy-start | bytes 19204
  771.9 107.9 %collective-permute-start.1 = (bf16[1600,256]{1,0:T(8,128)(2,1)}, bf16[1600,256]{1,0:T(8,128)(2,1)}, u32[]{:S(2)}, u32[]{:S(2)}) collective-permute-start(bf16[1600,256]{1,0:T(8,128)(2,1)} %get-tuple-element.34), channel_id=1, source_target_pairs={{0,0},{8,1},{16,2},{24,3},{1,4},{9,5},{17,6},{25,7},{2,8},{10,9},{... | collective-permute-start | bytes 2457608 | tf_op jit(solution)/shard_map/ppermute | solution.py:53
  879.8 204.3 %all-to-all-start.3 = ((bf16[8,200,1,256]{3,1,2,0:T(8,128)(2,1)}), bf16[8,200,1,256]{3,1,2,0:T(8,128)(2,1)S(1)}, u32[]{:S(2)}, u32[]{:S(2)}) async-start(bf16[8,200,1,256]{3,1,2,0:T(8,128)(2,1)} %bitcast.65), calls=%async_computation.5 | async-start | bytes 1638400 | tf_op jit(solution)/shard_map/all_to_all | solution.py:56
  884.4 203.7 %collective-permute-start.2 = (f32[1600,256]{1,0:T(8,128)}, f32[1600,256]{1,0:T(8,128)}, u32[]{:S(2)}, u32[]{:S(2)}) collective-permute-start(f32[1600,256]{1,0:T(8,128)} %get-tuple-element.33), channel_id=1, source_target_pairs={{0,0},{8,1},{16,2},{24,3},{1,4},{9,5},{17,6},{25,7},{2,8},{10,9},{... | collective-permute-start | bytes 4915208 | tf_op jit(solution)/shard_map/ppermute | solution.py:53
  1084.1 12.2 all-to-all-start.5
  1097.1 357.2 %all-to-all-start.4 = ((f32[8,200,1,256]{3,1,2,0:T(8,128)}), f32[8,200,1,256]{3,1,2,0:T(8,128)S(1)}, u32[]{:S(2)}, u32[]{:S(2)}) async-start(f32[8,200,1,256]{3,1,2,0:T(8,128)} %bitcast.120), calls=%async_computation.8 | async-start | bytes 3276800 | tf_op jit(solution)/shard_map/all_to_all | solution.py:56
  1101.7 263.1 %copy-start.34 = (f32[1600]{0:T(1024)S(1)}, f32[1600]{0:T(1024)}, u32[]{:S(2)}) copy-start(f32[1600]{0:T(1024)} %get-tuple-element.76) | copy-start | bytes 19204
  1101.7 299.5 %copy-start.33 = (s32[400]{0:T(512)S(1)}, s32[400]{0:T(512)}, u32[]{:S(2)}) copy-start(s32[400]{0:T(512)} %copy-done.32) | copy-start | bytes 4804
  1362.5 89.4 %copy-start.37 = (s32[1200]{0:T(1024)S(1)}, s32[1200]{0:T(1024)}, u32[]{:S(2)}) copy-start(s32[1200]{0:T(1024)} %copy-done.36) | copy-start | bytes 14404
  (29 other events, 100.9 us)
Sparse Core Ops, SparseCore 0:
  23.4 148.3 all-gather.10
  191.8 49.7 all-gather.12
  244.3 44.4 all-gather.8
  294.0 37.1 reduce-scatter.14
  333.5 86.1 all-gather.16
  421.8 28.9 all-gather.14
  453.2 86.1 all-gather.18
  564.6 38.0 reduce-scatter.18
  608.3 29.6 all-gather.20
  687.0 38.7 reduce-scatter.20
  728.5 38.7 reduce-scatter.16
  770.6 101.1 reduce-scatter.22
  875.7 205.4 reduce-scatter.24
  1084.8 149.5 reduce-scatter.28
  1237.8 122.3 reduce-scatter.26
where the time goes:
time: 1470 us; the launch traced here: 1460 us
  waiting for transfers between devices  986 us (67%)
  blocking collectives  198 us (13%)
  matrix products  146 us (10%)
  other arithmetic  45.3 us (3%)
  local copies, waits for them, and re-layouts  40.1 us (3%)
  starting transfers between devices  31.4 us (2%)
  between operations  16.2 us (1%)
    unnamed x18, waiting for transfers between devices  450 us
    all_gather x4, waiting for transfers between devices, whole_weight(): return lax.all_gather(weight, 'row', axis=0, tiled=True)  167 us
    dot_general x58, matrix products, product(): lax.dot_general(left, right, dims, preferred_element_type=jnp.float32)  146 us
    ppermute x1, waiting for transfers between devices, to_blocks(): return lax.ppermute(got, ('row', 'col'), block_order(rows, cols))  103 us
    reduce_scatter x4, waiting for transfers between devices, share(): lax.psum_scatter(values.astype(jnp.bfloat16), 'col', scatter_dimension=1,...  102 us
    reduce_scatter x1, waiting for transfers between devices, share_weight(): lax.psum_scatter(gradient.astype(jnp.bfloat16), 'row', scatter_dimension=...  95.2 us
    all_to_all x1, blocking collectives, to_blocks(): got = lax.all_to_all(split, 'row', split_axis=2, concat_axis=1)  61.1 us
    all_gather x2, waiting for transfers between devices, spread(): return lax.all_gather(values, 'col', axis=1, tiled=True)  60.6 us
  transfers between devices with their start and end apart: 22, of which 14 were waited for; matrix products, arithmetic and copies ran while one was open for 9% of the time, Pallas kernels for 0%

commit v1 on v0

--- a/solution.py
+++ b/solution.py
@@ -139,7 +139,32 @@
 
 
 def whole_weight(weight):
-    return lax.all_gather(weight, "row", axis=0, tiled=True)
+
+    def supply_all_spans(xs, link_axis):
+        piece_next, mat_out, carry_in = (
+            lax.axis_size(link_axis),
+            lax.axis_index(link_axis),
+            xs.shape[0],
+        )
+        queue = tuple(((t, (t + 1) % piece_next) for t in range(piece_next)))
+        arrivals = tuple(((t, (t - 1) % piece_next) for t in range(piece_next)))
+        f_next = jnp.zeros((*xs.shape[:0], piece_next * carry_in, *xs.shape[1:]), xs.dtype)
+        f_next = lax.dynamic_update_slice_in_dim(f_next, xs, mat_out * carry_in, axis=0)
+        current_value = local_next = xs
+        block_last = piece_next // 2
+        for m in [*range(1, block_last + 1)]:
+            current_value = lax.ppermute(current_value, link_axis, queue)
+            f_next = lax.dynamic_update_slice_in_dim(
+                f_next, current_value, (mat_out - m) % piece_next * carry_in, axis=0
+            )
+            if m < piece_next - block_last:
+                local_next = lax.ppermute(local_next, link_axis, arrivals)
+                f_next = lax.dynamic_update_slice_in_dim(
+                    f_next, local_next, (mat_out + m) % piece_next * carry_in, axis=0
+                )
+        return f_next
+
+    return supply_all_spans(weight, "row")
 
 
 def share_weight(gradient):

time: 1470 us -> 1630 us (1.11)
  local copies, waits for them, and re-layouts: 40.1 us -> 135 us
  starting transfers between devices: 31.4 us -> 74 us
  waiting for transfers between devices: 986 us -> 1010 us
    ppermute x0 -> x28, waiting for transfers between devices: none -> 248 us  [the longest x12 154 us: supply_all_spans(): local_next = lax.ppermute(local_next, link_axis, arrivals)]
    all_gather x4 -> x0, waiting for transfers between devices: 167 us -> none  [whole_weight(): return lax.all_gather(weight, 'row', axis=0, tiled=True)]
    dynamic_update_slice x0 -> x32, local copies, waits for them, and re-layouts: none -> 85.7 us  [the longest x16 41.9 us: supply_all_spans(): lax.dynamic_update_slice_in_dim(f_next, current_value, (mat_out - m) % pi...]
    ppermute x0 -> x28, starting transfers between devices: none -> 42.8 us  [the longest x12 25.8 us: supply_all_spans(): local_next = lax.ppermute(local_next, link_axis, arrivals)]
    all_gather x2, waiting for transfers between devices: 60.6 us -> 29.3 us  [spread(): return lax.all_gather(values, 'col', axis=1, tiled=True)]
    ppermute x1, waiting for transfers between devices: 103 us -> 71.3 us  [to_blocks(): return lax.ppermute(got, ('row', 'col'), block_order(rows, cols))]
    all_to_all x1, blocking collectives: 61.1 us -> 42.8 us  [to_blocks(): got = lax.all_to_all(split, 'row', split_axis=2, concat_axis=1)]
    unnamed x18 -> x14, waiting for transfers between devices: 450 us -> 450 us
  transfers between devices with their start and end apart: 22 -> 46, of which waited for: 14 -> 22; matrix products, arithmetic and copies ran while one was open for 9% -> 11% of each run, Pallas kernels for 0% -> 0%
where the time goes in v1:
time: 1630 us; the launch traced here: 1620 us
  waiting for transfers between devices  1010 us (62%)
  blocking collectives  193 us (12%)
  matrix products  147 us (9%)
  local copies, waits for them, and re-layouts  135 us (8%)
  starting transfers between devices  74 us (5%)
  other arithmetic  45 us (3%)
  between operations  16.3 us (1%)
    unnamed x14, waiting for transfers between devices  450 us
    ppermute x12, waiting for transfers between devices, supply_all_spans(): local_next = lax.ppermute(local_next, link_axis, arrivals)  154 us
    dot_general x58, matrix products, product(): lax.dot_general(left, right, dims, preferred_element_type=jnp.float32)  147 us
    reduce_scatter x4, waiting for transfers between devices, share(): lax.psum_scatter(values.astype(jnp.bfloat16), 'col', scatter_dimension=1,...  107 us
    reduce_scatter x1, waiting for transfers between devices, share_weight(): lax.psum_scatter(gradient.astype(jnp.bfloat16), 'row', scatter_dimension=...  95.4 us
    ppermute x16, waiting for transfers between devices, supply_all_spans(): current_value = lax.ppermute(current_value, link_axis, queue)  93.9 us
    ppermute x1, waiting for transfers between devices, to_blocks(): return lax.ppermute(got, ('row', 'col'), block_order(rows, cols))  71.3 us
    psum x1, blocking collectives, body(): features = lax.psum(features, ('row', 'col'))  46 us
  transfers between devices with their start and end apart: 46, of which 22 were waited for; matrix products, arithmetic and copies ran while one was open for 11% of the time, Pallas kernels for 0%

profile of v1, /device:TPU:14, one launch (start us, length us, event | category | flops | bytes accessed | tf_op | source)
XLA Modules:
  0.0 1620.5 jit_solution(14455313976478105312)
XLA Ops:
  10.5 42.8 %all_to_all.65 = bf16[2,1,200,8,256]{4,2,0,1,3:T(8,128)(2,1)S(1)} all-to-all(bf16[2,1,200,8,256]{4,2,0,1,3:T(8,128)(2,1)S(1)} %copy.120), channel_id=1, replica_groups=mesh['row'=8,'col'=4] {'row'}, dimensions={3} | all-to-all | bytes 3276800 | tf_op jit(solution)/shard_map/all_to_all | solution.py:46
  55.7 71.3 %collective-permute-done = bf16[2,1600,256]{2,1,0:T(8,128)(2,1)S(1)} collective-permute-done((bf16[2,1600,256]{2,1,0:T(8,128)(2,1)S(1)}, bf16[2,1600,256]{2,1,0:T(8,128)(2,1)S(1)}, u32[]{:S(2)}, u32[]{:S(2)}) %collective-permute-start) | collective-permute-done | bytes 1638432 | tf_op jit(solution)/shard_map/ppermute | solution.py:48
  131.2 22.6 %all_to_all.66 = bf16[200,4,336]{2,0,1:T(8,128)(2,1)S(1)} all-to-all(bf16[200,4,336]{2,0,1:T(8,128)(2,1)S(1)} %copy.124), channel_id=1, replica_groups=mesh['row'=8,'col'=4] {'col'}, dimensions={1} | all-to-all | bytes 1075200 | tf_op jit(solution)/shard_map/all_to_all | solution.py:72
  156.5 25.6 %collective-permute-done.8 = bf16[200,1344]{1,0:T(8,128)(2,1)S(1)} collective-permute-done((bf16[200,1344]{1,0:T(8,128)(2,1)S(1)}, bf16[200,1344]{1,0:T(8,128)(2,1)S(1)}, u32[]{:S(2)}, u32[]{:S(2)}) %collective-permute-start.8) | collective-permute-done | bytes 537632 | tf_op jit(solution)/shard_map/ppermute | solution.py:156
  185.5 5.4 all-to-all-start.1
  191.0 30.3 %all-gather = f32[8,200,6]{1,2,0:T(8,128)S(1)} all-gather(f32[1,200,6]{1,2,0:T(8,128)S(1)} %bitcast.490), channel_id=1, replica_groups=mesh['row'=8,'col'=4] {'row'}, dimensions={0}, use_global_device_ids=true | all-gather | bytes 43200 | tf_op jit(solution)/shard_map/all_gather | solution.py:195
  223.0 10.2 all-reduce.1
  242.6 28.8 %collective-permute-done.2 = bf16[200,448]{1,0:T(8,128)(2,1)} collective-permute-done((bf16[200,448]{1,0:T(8,128)(2,1)S(1)}, bf16[200,448]{1,0:T(8,128)(2,1)}, u32[]{:S(2)}, u32[]{:S(2)}) %collective-permute-start.2) | collective-permute-done | bytes 179232 | tf_op jit(solution)/shard_map/ppermute | solution.py:161
  279.0 8.6 dynamic_update_slice.104
  294.4 16.1 collective-permute-done.5
  312.3 14.5 collective-permute-done.7
  327.1 8.8 dynamic_update_slice.105
  337.2 8.6 dynamic_update_slice.106
  347.2 8.7 dynamic_update_slice.107
  357.2 8.6 dynamic_update_slice.108
  367.1 7.7 dynamic_update_slice.109
  376.2 8.7 dynamic_update_slice.110
  386.2 8.5 dynamic_update_slice.111
  400.4 7.7 fusion.38
  431.3 40.7 %reduce-scatter.15.cloned.1.call-done = bf16[1600,256]{1,0:T(8,128)(2,1)} async-done(((bf16[1600,1024]{1,0:T(8,128)(2,1)}), bf16[1600,256]{1,0:T(8,128)(2,1)}) %reduce-scatter.15.cloned.1.call-update) | async-done | bytes 819216 | tf_op jit(solution)/shard_map/reduce_scatter | solution.py:136
  491.3 31.4 %collective-permute-done.23 = bf16[200,1600]{1,0:T(8,128)(2,1)S(1)} collective-permute-done((bf16[200,1600]{1,0:T(8,128)(2,1)S(1)}, bf16[200,1600]{1,0:T(8,128)(2,1)S(1)}, u32[]{:S(2)}, u32[]{:S(2)}) %collective-permute-start.23) | collective-permute-done | bytes 640032 | tf_op jit(solution)/shard_map/ppermute | solution.py:161
  526.1 25.1 %collective-permute-done.16 = bf16[200,1600]{1,0:T(8,128)(2,1)S(1)} collective-permute-done((bf16[200,1600]{1,0:T(8,128)(2,1)S(1)}, bf16[200,1600]{1,0:T(8,128)(2,1)S(1)}, u32[]{:S(2)}, u32[]{:S(2)}) %collective-permute-start.16) | collective-permute-done | bytes 640032 | tf_op jit(solution)/shard_map/ppermute | solution.py:161
  558.2 21.5 %collective-permute-done.25 = bf16[200,1600]{1,0:T(8,128)(2,1)S(1)} collective-permute-done((bf16[200,1600]{1,0:T(8,128)(2,1)S(1)}, bf16[200,1600]{1,0:T(8,128)(2,1)S(1)}, u32[]{:S(2)}, u32[]{:S(2)}) %collective-permute-start.25) | collective-permute-done | bytes 640032 | tf_op jit(solution)/shard_map/ppermute | solution.py:161
  583.1 25.1 %collective-permute-done.18 = bf16[200,1600]{1,0:T(8,128)(2,1)S(1)} collective-permute-done((bf16[200,1600]{1,0:T(8,128)(2,1)S(1)}, bf16[200,1600]{1,0:T(8,128)(2,1)S(1)}, u32[]{:S(2)}, u32[]{:S(2)}) %collective-permute-start.18) | collective-permute-done | bytes 640032 | tf_op jit(solution)/shard_map/ppermute | solution.py:161
  615.2 23.4 %collective-permute-done.26 = bf16[200,1600]{1,0:T(8,128)(2,1)S(1)} collective-permute-done((bf16[200,1600]{1,0:T(8,128)(2,1)S(1)}, bf16[200,1600]{1,0:T(8,128)(2,1)S(1)}, u32[]{:S(2)}, u32[]{:S(2)}) %collective-permute-start.26) | collective-permute-done | bytes 640032 | tf_op jit(solution)/shard_map/ppermute | solution.py:156
  639.1 13.8 collective-permute-done.19
  656.0 22.4 %collective-permute-done.20 = bf16[200,1600]{1,0:T(8,128)(2,1)S(1)} collective-permute-done((bf16[200,1600]{1,0:T(8,128)(2,1)S(1)}, bf16[200,1600]{1,0:T(8,128)(2,1)S(1)}, u32[]{:S(2)}, u32[]{:S(2)}) %collective-permute-start.20) | collective-permute-done | bytes 640032 | tf_op jit(solution)/shard_map/ppermute | solution.py:161
  681.5 9.8 fusion.226
  691.4 17.0 %convert_reduce_fusion.1 = (f32[1600]{0:T(1024)}, bf16[1600,1024]{1,0:T(8,128)(2,1)S(1)}) fusion(f32[1600,1024]{1,0:T(8,128)S(1)} %fusion.226, f32[1600]{0:T(1024)S(1)} %copy-done.53, bf16[1600,1600]{1,0:T(8,128)(2,1)} %constant_dynamic-update-slice_fusion.22, bf16[2,1600,1024]{2,1,0:T(8,128)(2,1)} %all-gather.5.cloned.1.call-done), kind=kOutput, calls=%fused_computation.25 | convolution fusion | flops 5280561664 | bytes 18444800 | tf_op jit(solution)/shard_map/dot_general | solution.py:19
  710.2 10.1 convolution_convert_fusion.4
  720.6 39.1 %reduce-scatter.19.cloned.1.call-done = bf16[1600,256]{1,0:T(8,128)(2,1)} async-done(((bf16[1600,1024]{1,0:T(8,128)(2,1)}), bf16[1600,256]{1,0:T(8,128)(2,1)}) %reduce-scatter.19.cloned.1.call-update) | async-done | bytes 819216 | tf_op jit(solution)/shard_map/reduce_scatter | solution.py:136
  765.8 29.3 %all-gather.9.cloned.1.call-done = bf16[1600,1024]{1,0:T(8,128)(2,1)} async-done(((bf16[1600,256]{1,0:T(8,128)(2,1)}), bf16[1600,1024]{1,0:T(8,128)(2,1)}) %all-gather.9.cloned.1.call-update) | async-done | bytes 3276816 | tf_op jit(solution)/shard_map/all_gather | solution.py:132
  837.1 6.8 convolution_convert_fusion.3
  843.9 11.5 convolution_convert_fusion.5
  855.6 5.4 convolution_convert_fusion.7
  861.1 9.7 convolution_convert_fusion.2
  871.3 13.0 convolution_convert_fusion
  884.4 10.2 convolution_convert_fusion.1
  897.0 27.3 %reduce-scatter.17.cloned.1.call-done = bf16[1600,256]{1,0:T(8,128)(2,1)} async-done(((bf16[1600,1024]{1,0:T(8,128)(2,1)}), bf16[1600,256]{1,0:T(8,128)(2,1)}) %reduce-scatter.17.cloned.1.call-update) | async-done | bytes 819216 | tf_op jit(solution)/shard_map/reduce_scatter | solution.py:136
  933.6 95.4 %reduce-scatter.23.cloned.1.call-done = bf16[200,448]{1,0:T(8,128)(2,1)} async-done(((bf16[1600,448]{1,0:T(8,128)(2,1)}), bf16[200,448]{1,0:T(8,128)(2,1)}) %reduce-scatter.23.cloned.1.call-update) | async-done | bytes 179216 | tf_op jit(solution)/shard_map/reduce_scatter | solution.py:171
  1030.2 6.9 all_to_all.67
  1046.0 192.3 %reduce-scatter.25.cloned.1.call-done = bf16[200,1344]{1,0:T(8,128)(2,1)} async-done(((bf16[1600,1344]{1,0:T(8,128)(2,1)}), bf16[200,1344]{1,0:T(8,128)(2,1)}) %reduce-scatter.25.cloned.1.call-update) | async-done | bytes 537616
  1245.3 8.1 all-to-all-done.5
  1258.9 132.7 %reduce-scatter.29.cloned.1.call-done = bf16[200,1600]{1,0:T(8,128)(2,1)} async-done(((bf16[1600,1600]{1,0:T(8,128)(2,1)}), bf16[200,1600]{1,0:T(8,128)(2,1)}) %reduce-scatter.29.cloned.1.call-update) | async-done | bytes 640016
  1393.8 124.5 %reduce-scatter.27.cloned.1.call-done = bf16[200,1600]{1,0:T(8,128)(2,1)} async-done(((bf16[1600,1600]{1,0:T(8,128)(2,1)}), bf16[200,1600]{1,0:T(8,128)(2,1)}) %reduce-scatter.27.cloned.1.call-update) | async-done | bytes 640016
  1522.9 29.2 %psum.15 = f32[2944]{0:T(1024)S(1)} all-reduce(f32[2944]{0:T(1024)S(1)} %pad_maximum_fusion.8), channel_id=1, replica_groups=mesh['row'=8,'col'=4] {'row'}, use_global_device_ids=true, to_apply=%region_45.46 | all-reduce | flops 2944 | bytes 23552 | tf_op jit(solution)/shard_map/psum | solution.py:273
  1552.8 5.3 all_gather.23
  1560.5 46.0 %psum.14 = f32[6,1600]{1,0:T(8,128)S(1)} all-reduce(f32[6,1600]{1,0:T(8,128)S(1)} %stack.110), channel_id=1, replica_groups=mesh['row'=8,'col'=4] {'row','col'}, use_global_device_ids=true, to_apply=%region_41.42 | all-reduce | flops 9600 | bytes 76800 | tf_op jit(solution)/shard_map/psum | solution.py:271
  (408 shorter events, 227.3 us)
Async XLA Ops:
  7.2 387.5 %all-gather.5.cloned.1.call-start = ((), (), s32[]{:S(2)}) async-start(), calls=%async_computation.15 | async-start | bytes 8192000 | tf_op jit(solution)/shard_map/all_gather | solution.py:212
  53.4 73.6 %collective-permute-start = (bf16[2,1600,256]{2,1,0:T(8,128)(2,1)S(1)}, bf16[2,1600,256]{2,1,0:T(8,128)(2,1)S(1)}, u32[]{:S(2)}, u32[]{:S(2)}) collective-permute-start(bf16[2,1600,256]{2,1,0:T(8,128)(2,1)S(1)} %bitcast.453), channel_id=1, source_target_pairs={{0,0},{1,8},{2,16},{3,24},{4,1},{5,9},{6,17},{7,25},{8,2},{9,10},{... | collective-permute-start | bytes 4915208 | tf_op jit(solution)/shard_map/ppermute | solution.py:48
  154.5 27.7 %collective-permute-start.8 = (bf16[200,1344]{1,0:T(8,128)(2,1)S(1)}, bf16[200,1344]{1,0:T(8,128)(2,1)S(1)}, u32[]{:S(2)}, u32[]{:S(2)}) collective-permute-start(bf16[200,1344]{1,0:T(8,128)(2,1)S(1)} %reshape.542), channel_id=1, source_target_pairs={{0,4},{4,8},{8,12},{12,16},{16,20},{20,24},{24,28},{28,0},{1,5},{5... | collective-permute-start | bytes 1612808 | tf_op jit(solution)/shard_map/ppermute | solution.py:156
  154.5 79.0 %collective-permute-start.9 = (bf16[200,1344]{1,0:T(8,128)(2,1)S(1)}, bf16[200,1344]{1,0:T(8,128)(2,1)}, u32[]{:S(2)}, u32[]{:S(2)}) collective-permute-start(bf16[200,1344]{1,0:T(8,128)(2,1)S(1)} %reshape.542), channel_id=1, source_target_pairs={{0,28},{4,0},{8,4},{12,8},{16,12},{20,16},{24,20},{28,24},{1,29},{... | collective-permute-start | bytes 1612808 | tf_op jit(solution)/shard_map/ppermute | solution.py:161
  182.2 56.3 %collective-permute-start.10 = (bf16[200,1344]{1,0:T(8,128)(2,1)S(1)}, bf16[200,1344]{1,0:T(8,128)(2,1)}, u32[]{:S(2)}, u32[]{:S(2)}) collective-permute-start(bf16[200,1344]{1,0:T(8,128)(2,1)S(1)} %collective-permute-done.8), channel_id=1, source_target_pairs={{0,4},{4,8},{8,12},{12,16},{16,20},{20,24},{24,28},{28,0},{1,5},{5... | collective-permute-start | bytes 1612808 | tf_op jit(solution)/shard_map/ppermute | solution.py:156
  185.5 53.1 %all-to-all-start.1 = ((bf16[200,4,112]{2,0,1:T(8,128)(2,1)}), bf16[200,4,112]{2,0,1:T(8,128)(2,1)S(1)}, u32[]{:S(2)}, u32[]{:S(2)}) async-start(bf16[200,4,112]{2,0,1:T(8,128)(2,1)} %copy.122), calls=%async_computation.1 | async-start | bytes 409600 | tf_op jit(solution)/shard_map/all_to_all | solution.py:72
  190.9 281.1 %reduce-scatter.15.cloned.1.call-start = ((), (), s32[]{:S(2)}) async-start(), calls=%async_computation.16 | async-start | bytes 4096000 | tf_op jit(solution)/shard_map/reduce_scatter | solution.py:136
  233.5 57.0 %collective-permute-start.11 = (bf16[200,1344]{1,0:T(8,128)(2,1)}, bf16[200,1344]{1,0:T(8,128)(2,1)}, u32[]{:S(2)}, u32[]{:S(2)}) collective-permute-start(bf16[200,1344]{1,0:T(8,128)(2,1)} %collective-permute-done.9), channel_id=1, source_target_pairs={{0,28},{4,0},{8,4},{12,8},{16,12},{20,16},{24,20},{28,24},{1,29},{... | collective-permute-start | bytes 1612808 | tf_op jit(solution)/shard_map/ppermute | solution.py:161
  238.5 53.9 %collective-permute-start.12 = (bf16[200,1344]{1,0:T(8,128)(2,1)}, bf16[200,1344]{1,0:T(8,128)(2,1)}, u32[]{:S(2)}, u32[]{:S(2)}) collective-permute-start(bf16[200,1344]{1,0:T(8,128)(2,1)} %collective-permute-done.10), channel_id=1, source_target_pairs={{0,4},{4,8},{8,12},{12,16},{16,20},{20,24},{24,28},{28,0},{1,5},{5... | collective-permute-start | bytes 1612808 | tf_op jit(solution)/shard_map/ppermute | solution.py:156
  238.8 32.5 %collective-permute-start.2 = (bf16[200,448]{1,0:T(8,128)(2,1)S(1)}, bf16[200,448]{1,0:T(8,128)(2,1)}, u32[]{:S(2)}, u32[]{:S(2)}) collective-permute-start(bf16[200,448]{1,0:T(8,128)(2,1)S(1)} %reshape.540), channel_id=1, source_target_pairs={{0,28},{4,0},{8,4},{12,8},{16,12},{20,16},{24,20},{28,24},{1,29},{... | collective-permute-start | bytes 537608 | tf_op jit(solution)/shard_map/ppermute | solution.py:161
  240.9 33.1 %collective-permute-start.1 = (bf16[200,448]{1,0:T(8,128)(2,1)S(1)}, bf16[200,448]{1,0:T(8,128)(2,1)}, u32[]{:S(2)}, u32[]{:S(2)}) collective-permute-start(bf16[200,448]{1,0:T(8,128)(2,1)S(1)} %reshape.540), channel_id=1, source_target_pairs={{0,4},{4,8},{8,12},{12,16},{16,20},{20,24},{24,28},{28,0},{1,5},{5... | collective-permute-start | bytes 537608 | tf_op jit(solution)/shard_map/ppermute | solution.py:156
  271.4 16.2 %collective-permute-start.4 = (bf16[200,448]{1,0:T(8,128)(2,1)}, bf16[200,448]{1,0:T(8,128)(2,1)}, u32[]{:S(2)}, u32[]{:S(2)}) collective-permute-start(bf16[200,448]{1,0:T(8,128)(2,1)} %collective-permute-done.2), channel_id=1, source_target_pairs={{0,28},{4,0},{8,4},{12,8},{16,12},{20,16},{24,20},{28,24},{1,29},{... | collective-permute-start | bytes 537608 | tf_op jit(solution)/shard_map/ppermute | solution.py:161
  274.0 15.5 collective-permute-start.3
  287.6 24.6 %collective-permute-start.6 = (bf16[200,448]{1,0:T(8,128)(2,1)}, bf16[200,448]{1,0:T(8,128)(2,1)S(1)}, u32[]{:S(2)}, u32[]{:S(2)}) collective-permute-start(bf16[200,448]{1,0:T(8,128)(2,1)} %collective-permute-done.4), channel_id=1, source_target_pairs={{0,28},{4,0},{8,4},{12,8},{16,12},{20,16},{24,20},{28,24},{1,29},{... | collective-permute-start | bytes 537608 | tf_op jit(solution)/shard_map/ppermute | solution.py:161
  289.4 21.2 %collective-permute-start.5 = (bf16[200,448]{1,0:T(8,128)(2,1)S(1)}, bf16[200,448]{1,0:T(8,128)(2,1)S(1)}, u32[]{:S(2)}, u32[]{:S(2)}) collective-permute-start(bf16[200,448]{1,0:T(8,128)(2,1)S(1)} %collective-permute-done.3), channel_id=1, source_target_pairs={{0,4},{4,8},{8,12},{12,16},{16,20},{20,24},{24,28},{28,0},{1,5},{5... | collective-permute-start | bytes 537608 | tf_op jit(solution)/shard_map/ppermute | solution.py:156
  290.5 84.3 %collective-permute-start.13 = (bf16[200,1344]{1,0:T(8,128)(2,1)}, bf16[200,1344]{1,0:T(8,128)(2,1)}, u32[]{:S(2)}, u32[]{:S(2)}) collective-permute-start(bf16[200,1344]{1,0:T(8,128)(2,1)} %collective-permute-done.11), channel_id=1, source_target_pairs={{0,28},{4,0},{8,4},{12,8},{16,12},{20,16},{24,20},{28,24},{1,29},{... | collective-permute-start | bytes 1612808 | tf_op jit(solution)/shard_map/ppermute | solution.py:161
  292.4 92.4 %collective-permute-start.14 = (bf16[200,1344]{1,0:T(8,128)(2,1)}, bf16[200,1344]{1,0:T(8,128)(2,1)}, u32[]{:S(2)}, u32[]{:S(2)}) collective-permute-start(bf16[200,1344]{1,0:T(8,128)(2,1)} %collective-permute-done.12), channel_id=1, source_target_pairs={{0,4},{4,8},{8,12},{12,16},{16,20},{20,24},{24,28},{28,0},{1,5},{5... | collective-permute-start | bytes 1612808 | tf_op jit(solution)/shard_map/ppermute | solution.py:156
  310.6 16.2 %collective-permute-start.7 = (bf16[200,448]{1,0:T(8,128)(2,1)S(1)}, bf16[200,448]{1,0:T(8,128)(2,1)S(1)}, u32[]{:S(2)}, u32[]{:S(2)}) collective-permute-start(bf16[200,448]{1,0:T(8,128)(2,1)S(1)} %collective-permute-done.5), channel_id=1, source_target_pairs={{0,4},{4,8},{8,12},{12,16},{16,20},{20,24},{24,28},{28,0},{1,5},{5... | collective-permute-start | bytes 537608 | tf_op jit(solution)/shard_map/ppermute | solution.py:156
  431.2 250.3 %all-gather.7.cloned.1.call-start = ((), (), s32[]{:S(2)}) async-start(), calls=%async_computation.17 | async-start | bytes 4096000 | tf_op jit(solution)/shard_map/all_gather | solution.py:132
  478.0 281.8 %reduce-scatter.19.cloned.1.call-start = ((), (), s32[]{:S(2)}) async-start(), calls=%async_computation.19 | async-start | bytes 4096000 | tf_op jit(solution)/shard_map/reduce_scatter | solution.py:136
  478.2 44.5 %collective-permute-start.23 = (bf16[200,1600]{1,0:T(8,128)(2,1)S(1)}, bf16[200,1600]{1,0:T(8,128)(2,1)S(1)}, u32[]{:S(2)}, u32[]{:S(2)}) collective-permute-start(bf16[200,1600]{1,0:T(8,128)(2,1)S(1)} %copy-done.26), channel_id=1, source_target_pairs={{0,28},{4,0},{8,4},{12,8},{16,12},{20,16},{24,20},{28,24},{1,29},{... | collective-permute-start | bytes 1920008 | tf_op jit(solution)/shard_map/ppermute | solution.py:161
  478.8 46.4 %collective-permute-start.22 = (bf16[200,1600]{1,0:T(8,128)(2,1)S(1)}, bf16[200,1600]{1,0:T(8,128)(2,1)S(1)}, u32[]{:S(2)}, u32[]{:S(2)}) collective-permute-start(bf16[200,1600]{1,0:T(8,128)(2,1)S(1)} %copy-done.26), channel_id=1, source_target_pairs={{0,4},{4,8},{8,12},{12,16},{16,20},{20,24},{24,28},{28,0},{1,5},{5... | collective-permute-start | bytes 1920008 | tf_op jit(solution)/shard_map/ppermute | solution.py:156
  481.2 70.0 %collective-permute-start.16 = (bf16[200,1600]{1,0:T(8,128)(2,1)S(1)}, bf16[200,1600]{1,0:T(8,128)(2,1)S(1)}, u32[]{:S(2)}, u32[]{:S(2)}) collective-permute-start(bf16[200,1600]{1,0:T(8,128)(2,1)S(1)} %copy-done.27), channel_id=1, source_target_pairs={{0,28},{4,0},{8,4},{12,8},{16,12},{20,16},{24,20},{28,24},{1,29},{... | collective-permute-start | bytes 1920008 | tf_op jit(solution)/shard_map/ppermute | solution.py:161
  481.2 72.5 %collective-permute-start.15 = (bf16[200,1600]{1,0:T(8,128)(2,1)S(1)}, bf16[200,1600]{1,0:T(8,128)(2,1)S(1)}, u32[]{:S(2)}, u32[]{:S(2)}) collective-permute-start(bf16[200,1600]{1,0:T(8,128)(2,1)S(1)} %copy-done.27), channel_id=1, source_target_pairs={{0,4},{4,8},{8,12},{12,16},{16,20},{20,24},{24,28},{28,0},{1,5},{5... | collective-permute-start | bytes 1920008 | tf_op jit(solution)/shard_map/ppermute | solution.py:156
  522.7 57.1 %collective-permute-start.25 = (bf16[200,1600]{1,0:T(8,128)(2,1)S(1)}, bf16[200,1600]{1,0:T(8,128)(2,1)S(1)}, u32[]{:S(2)}, u32[]{:S(2)}) collective-permute-start(bf16[200,1600]{1,0:T(8,128)(2,1)S(1)} %collective-permute-done.23), channel_id=1, source_target_pairs={{0,28},{4,0},{8,4},{12,8},{16,12},{20,16},{24,20},{28,24},{1,29},{... | collective-permute-start | bytes 1920008 | tf_op jit(solution)/shard_map/ppermute | solution.py:161
  525.2 57.1 %collective-permute-start.24 = (bf16[200,1600]{1,0:T(8,128)(2,1)S(1)}, bf16[200,1600]{1,0:T(8,128)(2,1)S(1)}, u32[]{:S(2)}, u32[]{:S(2)}) collective-permute-start(bf16[200,1600]{1,0:T(8,128)(2,1)S(1)} %collective-permute-done.22), channel_id=1, source_target_pairs={{0,4},{4,8},{8,12},{12,16},{16,20},{20,24},{24,28},{28,0},{1,5},{5... | collective-permute-start | bytes 1920008 | tf_op jit(solution)/shard_map/ppermute | solution.py:156
  551.2 57.1 %collective-permute-start.18 = (bf16[200,1600]{1,0:T(8,128)(2,1)S(1)}, bf16[200,1600]{1,0:T(8,128)(2,1)S(1)}, u32[]{:S(2)}, u32[]{:S(2)}) collective-permute-start(bf16[200,1600]{1,0:T(8,128)(2,1)S(1)} %collective-permute-done.16), channel_id=1, source_target_pairs={{0,28},{4,0},{8,4},{12,8},{16,12},{20,16},{24,20},{28,24},{1,29},{... | collective-permute-start | bytes 1920008 | tf_op jit(solution)/shard_map/ppermute | solution.py:161
  553.7 57.1 %collective-permute-start.17 = (bf16[200,1600]{1,0:T(8,128)(2,1)S(1)}, bf16[200,1600]{1,0:T(8,128)(2,1)S(1)}, u32[]{:S(2)}, u32[]{:S(2)}) collective-permute-start(bf16[200,1600]{1,0:T(8,128)(2,1)S(1)} %collective-permute-done.15), channel_id=1, source_target_pairs={{0,4},{4,8},{8,12},{12,16},{16,20},{20,24},{24,28},{28,0},{1,5},{5... | collective-permute-start | bytes 1920008 | tf_op jit(solution)/shard_map/ppermute | solution.py:156
  579.7 75.4 %collective-permute-start.27 = (bf16[200,1600]{1,0:T(8,128)(2,1)S(1)}, bf16[200,1600]{1,0:T(8,128)(2,1)S(1)}, u32[]{:S(2)}, u32[]{:S(2)}) collective-permute-start(bf16[200,1600]{1,0:T(8,128)(2,1)S(1)} %collective-permute-done.25), channel_id=1, source_target_pairs={{0,28},{4,0},{8,4},{12,8},{16,12},{20,16},{24,20},{28,24},{1,29},{... | collective-permute-start | bytes 1920008 | tf_op jit(solution)/shard_map/ppermute | solution.py:161
  582.2 56.4 %collective-permute-start.26 = (bf16[200,1600]{1,0:T(8,128)(2,1)S(1)}, bf16[200,1600]{1,0:T(8,128)(2,1)S(1)}, u32[]{:S(2)}, u32[]{:S(2)}) collective-permute-start(bf16[200,1600]{1,0:T(8,128)(2,1)S(1)} %collective-permute-done.24), channel_id=1, source_target_pairs={{0,4},{4,8},{8,12},{12,16},{16,20},{20,24},{24,28},{28,0},{1,5},{5... | collective-permute-start | bytes 1920008 | tf_op jit(solution)/shard_map/ppermute | solution.py:156
  608.3 70.2 %collective-permute-start.20 = (bf16[200,1600]{1,0:T(8,128)(2,1)S(1)}, bf16[200,1600]{1,0:T(8,128)(2,1)S(1)}, u32[]{:S(2)}, u32[]{:S(2)}) collective-permute-start(bf16[200,1600]{1,0:T(8,128)(2,1)S(1)} %collective-permute-done.18), channel_id=1, source_target_pairs={{0,28},{4,0},{8,4},{12,8},{16,12},{20,16},{24,20},{28,24},{1,29},{... | collective-permute-start | bytes 1920008 | tf_op jit(solution)/shard_map/ppermute | solution.py:161
  610.7 42.1 %collective-permute-start.19 = (bf16[200,1600]{1,0:T(8,128)(2,1)S(1)}, bf16[200,1600]{1,0:T(8,128)(2,1)S(1)}, u32[]{:S(2)}, u32[]{:S(2)}) collective-permute-start(bf16[200,1600]{1,0:T(8,128)(2,1)S(1)} %collective-permute-done.17), channel_id=1, source_target_pairs={{0,4},{4,8},{8,12},{12,16},{16,20},{20,24},{24,28},{28,0},{1,5},{5... | collective-permute-start | bytes 1920008 | tf_op jit(solution)/shard_map/ppermute | solution.py:156
  638.6 40.7 %collective-permute-start.28 = (bf16[200,1600]{1,0:T(8,128)(2,1)S(1)}, bf16[200,1600]{1,0:T(8,128)(2,1)S(1)}, u32[]{:S(2)}, u32[]{:S(2)}) collective-permute-start(bf16[200,1600]{1,0:T(8,128)(2,1)S(1)} %collective-permute-done.26), channel_id=1, source_target_pairs={{0,4},{4,8},{8,12},{12,16},{16,20},{20,24},{24,28},{28,0},{1,5},{5... | collective-permute-start | bytes 1920008 | tf_op jit(solution)/shard_map/ppermute | solution.py:156
  652.9 27.7 %collective-permute-start.21 = (bf16[200,1600]{1,0:T(8,128)(2,1)S(1)}, bf16[200,1600]{1,0:T(8,128)(2,1)S(1)}, u32[]{:S(2)}, u32[]{:S(2)}) collective-permute-start(bf16[200,1600]{1,0:T(8,128)(2,1)S(1)} %collective-permute-done.19), channel_id=1, source_target_pairs={{0,4},{4,8},{8,12},{12,16},{16,20},{20,24},{24,28},{28,0},{1,5},{5... | collective-permute-start | bytes 1920008 | tf_op jit(solution)/shard_map/ppermute | solution.py:156
  720.3 74.8 %all-gather.9.cloned.1.call-start = ((), (), s32[]{:S(2)}) async-start(), calls=%async_computation.20 | async-start | bytes 4096000 | tf_op jit(solution)/shard_map/all_gather | solution.py:132
  765.3 129.4 %reduce-scatter.21.cloned.1.call-start = ((), (), s32[]{:S(2)}) async-start(), calls=%async_computation.21 | async-start | bytes 4096000 | tf_op jit(solution)/shard_map/reduce_scatter | solution.py:136
  843.9 80.4 %reduce-scatter.17.cloned.1.call-start = ((), (), s32[]{:S(2)}) async-start(), calls=%async_computation.18 | async-start | bytes 4096000 | tf_op jit(solution)/shard_map/reduce_scatter | solution.py:136
  855.5 173.5 %reduce-scatter.23.cloned.1.call-start = ((), (), s32[]{:S(2)}) async-start(), calls=%async_computation.22 | async-start | bytes 1843200 | tf_op jit(solution)/shard_map/reduce_scatter | solution.py:171
  861.0 377.3 %reduce-scatter.25.cloned.1.call-start = ((), (), s32[]{:S(2)}) async-start(), calls=%async_computation.23 | async-start | bytes 5068800
  870.8 520.7 %reduce-scatter.29.cloned.1.call-start = ((), (), s32[]{:S(2)}) async-start(), calls=%async_computation.25 | async-start | bytes 5990400
  884.3 633.9 %reduce-scatter.27.cloned.1.call-start = ((), (), s32[]{:S(2)}) async-start(), calls=%async_computation.24 | async-start | bytes 5990400
  929.0 108.1 %collective-permute-start.29 = (bf16[1600,256]{1,0:T(8,128)(2,1)}, bf16[1600,256]{1,0:T(8,128)(2,1)}, u32[]{:S(2)}, u32[]{:S(2)}) collective-permute-start(bf16[1600,256]{1,0:T(8,128)(2,1)} %get-tuple-element.34), channel_id=1, source_target_pairs={{0,0},{8,1},{16,2},{24,3},{1,4},{9,5},{17,6},{25,7},{2,8},{10,9},{... | collective-permute-start | bytes 2457608 | tf_op jit(solution)/shard_map/ppermute | solution.py:53
  1037.0 204.3 %all-to-all-start.3 = ((bf16[8,200,1,256]{3,1,2,0:T(8,128)(2,1)}), bf16[8,200,1,256]{3,1,2,0:T(8,128)(2,1)S(1)}, u32[]{:S(2)}, u32[]{:S(2)}) async-start(bf16[8,200,1,256]{3,1,2,0:T(8,128)(2,1)} %bitcast.63), calls=%async_computation.5 | async-start | bytes 1638400 | tf_op jit(solution)/shard_map/all_to_all | solution.py:56
  1041.6 203.8 %collective-permute-start.30 = (f32[1600,256]{1,0:T(8,128)}, f32[1600,256]{1,0:T(8,128)}, u32[]{:S(2)}, u32[]{:S(2)}) collective-permute-start(f32[1600,256]{1,0:T(8,128)} %get-tuple-element.33), channel_id=1, source_target_pairs={{0,0},{8,1},{16,2},{24,3},{1,4},{9,5},{17,6},{25,7},{2,8},{10,9},{... | collective-permute-start | bytes 4915208 | tf_op jit(solution)/shard_map/ppermute | solution.py:53
  1241.3 12.2 all-to-all-start.5
  1254.3 358.1 %all-to-all-start.4 = ((f32[8,200,1,256]{3,1,2,0:T(8,128)}), f32[8,200,1,256]{3,1,2,0:T(8,128)S(1)}, u32[]{:S(2)}, u32[]{:S(2)}) async-start(f32[8,200,1,256]{3,1,2,0:T(8,128)} %bitcast.116), calls=%async_computation.8 | async-start | bytes 3276800 | tf_op jit(solution)/shard_map/all_to_all | solution.py:56
  1258.8 264.0 %copy-start.38 = (f32[1600]{0:T(1024)S(1)}, f32[1600]{0:T(1024)}, u32[]{:S(2)}) copy-start(f32[1600]{0:T(1024)} %get-tuple-element.76) | copy-start | bytes 19204
  1258.8 300.4 %copy-start.37 = (s32[400]{0:T(512)S(1)}, s32[400]{0:T(512)}, u32[]{:S(2)}) copy-start(s32[400]{0:T(512)} %copy-done.36) | copy-start | bytes 4804
  (57 other events, 1732.7 us)
Sparse Core Ops, SparseCore 0:
  128.3 60.4 all-gather.4
  431.4 40.6 reduce-scatter.14
  478.1 29.6 all-gather.6
  720.4 39.3 reduce-scatter.18
  765.4 29.6 all-gather.8
  844.0 38.7 reduce-scatter.20
  885.6 38.7 reduce-scatter.16
  927.8 101.2 reduce-scatter.22
  1032.9 205.3 reduce-scatter.24
  1242.0 149.5 reduce-scatter.28
  1395.0 123.1 reduce-scatter.26
